TPU v7x, 32 devices: a whole 2x2x4 slice. The times are simulated.
32 devices in a mesh: expert: 4 (over y, x), tensor: 2 (over core), dp: 4 (over z).
Axes of the slice: x: 2, y: 2, z: 4, core: 2. Of those that a mesh axis runs over, the one named last changes fastest.
Arguments:
- tokens: bfloat16 [2048, 3072], P(('expert', 'dp'), 'tensor'), may hold values from -6 to 6
- experts_chosen: int32 [2048, 2], P(('expert', 'dp')), may hold values from 0 to 3, all different within a row; in each aligned block of 128 rows (0 to 127, 128 to 255, ...) at most 73 rows name the same one
- route_weights: float32 [2048, 2], P(('expert', 'dp')), may hold values from 0.1 to 1
- cotangent: bfloat16 [2048, 3072], P(('expert', 'dp'), 'tensor'), may hold values from -6 to 6
- gate_weight: bfloat16 [4, 3072, 8192], P('expert', 'dp', 'tensor'), may hold values from -0.15625 to 0.15625
- up_weight: bfloat16 [4, 3072, 8192], P('expert', 'dp', 'tensor'), may hold values from -0.15625 to 0.15625
- down_weight: bfloat16 [4, 8192, 3072], P('expert', 'tensor', 'dp'), may hold values from -0.09375 to 0.09375
Outputs:
- layer_output: bfloat16 [2048, 3072], P(('expert', 'dp'), 'tensor')
- token_grad: bfloat16 [2048, 3072], P(('expert', 'dp'), 'tensor')
- route_grad: float32 [2048, 2], P(('expert', 'dp'))
Inputs may be any that keep to these rules, and one draw needn't show every extreme that they name: `experts_chosen`: each row names 2 different experts. Among the 128 rows of one index of expert+dp no expert is named more than 73 times, and in some such block one expert is named exactly 73 times.
All inputs are finite; a program needn't handle non-finite values.
Results may differ from a plain program's by a relative error of at most 0.0072.
Values may be sent and summed in bfloat16 or wider, within the bound.
No kernel may reach another device: no remote copies, remote signals or barrier semaphores. Data moves between devices by JAX's collectives and lax.ppermute only.
A program may use at most 256 MiB of HBM per device.

v0:
```python
import jax
import jax.numpy as jnp
from jax import lax
from jax.sharding import PartitionSpec as P


def slot_table(experts_chosen, num_experts, cap_rows):
    flat_ids = experts_chosen.reshape(-1)
    expert_hot = (flat_ids[:, None] == jnp.arange(num_experts, dtype=jnp.int32)[None, :]).astype(
        jnp.int32
    )
    earlier = jnp.cumsum(expert_hot, axis=0) - expert_hot
    rank_slot = jnp.sum(earlier * expert_hot, axis=1)
    target = flat_ids * cap_rows + rank_slot
    all_slots = jnp.arange(num_experts * cap_rows, dtype=jnp.int32)
    return (target[:, None] == all_slots[None, :]).astype(jnp.bfloat16)


def to_slots(slot_onehot, pair_rows, num_experts, cap_rows):
    packed = jnp.einsum("ps,pd->sd", slot_onehot, pair_rows, preferred_element_type=jnp.float32)
    return packed.astype(jnp.bfloat16).reshape(num_experts, cap_rows, pair_rows.shape[1])


def from_slots(slot_onehot, returned):
    flat_back = returned.reshape(-1, returned.shape[2])
    return jnp.dot(slot_onehot, flat_back, preferred_element_type=jnp.float32)


def as_blocks(summed, num_experts, cap_rows):
    return summed.astype(jnp.bfloat16).reshape(num_experts, cap_rows, summed.shape[1])


def local(tokens, experts_chosen, route_weights, cotangent, gate_weight, up_weight, down_weight):
    tok_rows, feat_cols = tokens.shape
    top_count = experts_chosen.shape[1]
    num_experts = lax.axis_size("expert")
    cap_rows = min(tok_rows, 9 * tok_rows * top_count // (8 * num_experts) + 1)
    slot_onehot = slot_table(experts_chosen, num_experts, cap_rows)
    pair_weights = route_weights.reshape(-1, 1)
    token_pairs = jnp.repeat(tokens, top_count, axis=0)
    grad_pairs = (
        jnp.repeat(cotangent, top_count, axis=0).astype(jnp.float32) * pair_weights
    ).astype(jnp.bfloat16)
    token_send = to_slots(slot_onehot, token_pairs, num_experts, cap_rows)
    grad_send = to_slots(slot_onehot, grad_pairs, num_experts, cap_rows)
    token_recv = lax.all_to_all(token_send, "expert", split_axis=0, concat_axis=0, tiled=True)
    token_full = lax.all_gather(token_recv, "tensor", axis=2, tiled=True)
    model_cols = token_full.shape[2]
    token_rows = token_full.reshape(-1, model_cols)
    gate_all, up_all = (
        lax.all_gather(gate_weight, "dp", axis=1, tiled=True),
        lax.all_gather(up_weight, "dp", axis=1, tiled=True),
    )
    gate_pre = jnp.dot(token_rows, gate_all[0], preferred_element_type=jnp.float32)
    up_pre = jnp.dot(token_rows, up_all[0], preferred_element_type=jnp.float32)
    hidden = (jax.nn.silu(gate_pre) * up_pre).astype(jnp.bfloat16)
    down_all = lax.all_gather(down_weight, "dp", axis=2, tiled=True)
    out_part = jnp.dot(hidden, down_all[0], preferred_element_type=jnp.float32)
    out_sum = lax.psum_scatter(
        out_part.astype(jnp.bfloat16), "tensor", scatter_dimension=1, tiled=True
    ).astype(jnp.float32)
    out_back = lax.all_to_all(
        as_blocks(out_sum, num_experts, cap_rows), "expert", split_axis=0, concat_axis=0, tiled=True
    )
    grad_recv = lax.all_to_all(grad_send, "expert", split_axis=0, concat_axis=0, tiled=True)
    grad_full = lax.all_gather(grad_recv, "tensor", axis=2, tiled=True)
    grad_rows_all = grad_full.reshape(-1, model_cols)
    contract = (((1,), (1,)), ((), ()))
    hidden_grad = lax.dot_general(
        grad_rows_all, down_all[0], contract, preferred_element_type=jnp.float32
    )
    sigmoid_gate = jax.nn.sigmoid(gate_pre)
    up_grad = (hidden_grad * jax.nn.silu(gate_pre)).astype(jnp.bfloat16)
    gate_grad = (
        hidden_grad * up_pre * sigmoid_gate * (1.0 + gate_pre * (1.0 - sigmoid_gate))
    ).astype(jnp.bfloat16)
    in_part = lax.dot_general(gate_grad, gate_all[0], contract, preferred_element_type=jnp.float32)
    in_part = in_part + lax.dot_general(
        up_grad, up_all[0], contract, preferred_element_type=jnp.float32
    )
    in_sum = lax.psum_scatter(
        in_part.astype(jnp.bfloat16), "tensor", scatter_dimension=1, tiled=True
    ).astype(jnp.float32)
    in_back = lax.all_to_all(
        as_blocks(in_sum, num_experts, cap_rows), "expert", split_axis=0, concat_axis=0, tiled=True
    )
    out_pairs = from_slots(slot_onehot, out_back).reshape(tok_rows, top_count, feat_cols)
    in_pairs = from_slots(slot_onehot, in_back).reshape(tok_rows, top_count, feat_cols)
    layer_output = jnp.sum(route_weights[:, :, None] * out_pairs, axis=1).astype(jnp.bfloat16)
    token_grad = jnp.sum(in_pairs, axis=1).astype(jnp.bfloat16)
    local_dots = jnp.sum(cotangent.astype(jnp.float32)[:, None, :] * out_pairs, axis=2)
    route_grad = lax.psum(local_dots, "tensor")
    return (layer_output, token_grad, route_grad)


def solution(mesh):
    in_specs = (
        P(("expert", "dp"), "tensor"),
        P(("expert", "dp"), None),
        P(("expert", "dp"), None),
        P(("expert", "dp"), "tensor"),
        P("expert", "dp", "tensor"),
        P("expert", "dp", "tensor"),
        P("expert", "tensor", "dp"),
    )
    out_specs = (
        P(("expert", "dp"), "tensor"),
        P(("expert", "dp"), "tensor"),
        P(("expert", "dp"), None),
    )
    return jax.shard_map(local, mesh=mesh, in_specs=in_specs, out_specs=out_specs, check_vma=False)
```

profile of v0, /device:TPU:0, one launch (start us, length us, event | category | flops | bytes accessed | tf_op | source)
XLA Modules:
  0.0 1455.3 jit_solution(10602917999644850191)
XLA Ops:
  7.2 0.8 copy.21
  8.3 1.4 broadcast_in_dim.4
  10.1 1.2 reduce-window.6
  12.5 18.7 %all_to_all.20 = bf16[4,73,1536]{2,1,0:T(8,128)(2,1)} all-to-all(bf16[4,73,1536]{2,1,0:T(8,128)(2,1)S(1)} %reshape.107), channel_id=1, replica_groups=mesh['expert'=4,'tensor'=2,'dp'=4] {'expert'}, dimensions={0} | all-to-all | bytes 1794048 | tf_op jit(solution)/shard_map/all_to_all | solution.py:46
  31.7 1.1 convert_element_type.57
  33.0 0.5 convolution_convert_fusion
  33.8 15.7 %all_to_all.21 = bf16[4,73,1536]{2,1,0:T(8,128)(2,1)} all-to-all(bf16[4,73,1536]{2,1,0:T(8,128)(2,1)S(1)} %reshape.111), channel_id=1, replica_groups=mesh['expert'=4,'tensor'=2,'dp'=4] {'expert'}, dimensions={0} | all-to-all | bytes 1794048 | tf_op jit(solution)/shard_map/all_to_all | solution.py:65
  49.6 0.7 all-gather.10.cloned.1.call-update
  50.9 0.5 all-gather.12.cloned.1.call-update
  51.7 2.0 reshape.108
  53.7 5.9 all-gather.14.cloned.1.call-done
  59.6 3.3 reshape.112
  62.9 424.7 %all-gather.10.cloned.1.call-done = bf16[1,3072,4096]{2,1,0:T(8,128)(2,1)} async-done(((bf16[1,768,4096]{2,1,0:T(8,128)(2,1)}), bf16[1,3072,4096]{2,1,0:T(8,128)(2,1)}) %all-gather.10.cloned.1.call-update) | async-done | bytes 25165840 | tf_op jit(solution)/shard_map/all_gather | solution.py:52
  487.6 16.4 %fusion.6 = f32[292,4096]{1,0:T(8,128)} fusion(bf16[292,3072]{1,0:T(8,128)(2,1)S(1)} %reshape.108, bf16[1,3072,4096]{2,1,0:T(8,128)(2,1)} %all-gather.10.cloned.1.call-done), kind=kOutput, calls=%fused_computation.6 | convolution fusion | flops 7348420608 | bytes 31744000 | tf_op jit(solution)/shard_map/dot_general | solution.py:55
  504.0 408.4 %all-gather.8.cloned.1.call-done = bf16[1,3072,4096]{2,1,0:T(8,128)(2,1)} async-done(((bf16[1,768,4096]{2,1,0:T(8,128)(2,1)}), bf16[1,3072,4096]{2,1,0:T(8,128)(2,1)}) %all-gather.8.cloned.1.call-update) | async-done | bytes 25165840 | tf_op jit(solution)/shard_map/all_gather | solution.py:51
  912.4 16.3 %fusion.10 = f32[292,4096]{1,0:T(8,128)} fusion(bf16[292,3072]{1,0:T(8,128)(2,1)S(1)} %reshape.108, bf16[1,3072,4096]{2,1,0:T(8,128)(2,1)} %all-gather.8.cloned.1.call-done), kind=kOutput, calls=%fused_computation.10 | convolution fusion | flops 7348420608 | bytes 31744000 | tf_op jit(solution)/shard_map/dot_general | solution.py:54
  928.8 408.5 %all-gather.12.cloned.1.call-done = bf16[1,4096,3072]{2,1,0:T(8,128)(2,1)} async-done(((bf16[1,4096,768]{2,1,0:T(8,128)(2,1)}), bf16[1,4096,3072]{2,1,0:T(8,128)(2,1)}) %all-gather.12.cloned.1.call-update) | async-done | bytes 25165840 | tf_op jit(solution)/shard_map/all_gather | solution.py:57
  1337.3 14.5 fusion
  1351.7 16.7 %fusion.4 = f32[292,3072]{1,0:T(8,128)} fusion(bf16[1,3072,4096]{2,1,0:T(8,128)(2,1)} %all-gather.10.cloned.1.call-done, f32[292,4096]{1,0:T(8,128)} %fusion, f32[292,4096]{1,0:T(8,128)} %fusion.10), kind=kOutput, calls=%fused_computation.4 | convolution fusion | flops 7355596800 | bytes 38322176 | tf_op jit(solution)/shard_map/dot_general | solution.py:78
  1368.5 21.3 %fusion.16 = bf16[292,3072]{1,0:T(8,128)(2,1)} fusion(f32[292,3072]{1,0:T(8,128)} %fusion.4, bf16[1,3072,4096]{2,1,0:T(8,128)(2,1)} %all-gather.8.cloned.1.call-done, f32[292,4096]{1,0:T(8,128)} %fusion.10, f32[292,4096]{1,0:T(8,128)} %fusion, f32[292,4096]{1,0:T(8,128)} %fusion.6), kind=kOutput, calls=%fused_computation.18 | convolution fusion | flops 7362174976 | bytes 44900352 | tf_op jit(solution)/shard_map/dot_general | solution.py:77
  1389.9 17.2 %fusion.19 = bf16[292,3072]{1,0:T(8,128)(2,1)} fusion(bf16[1,4096,3072]{2,1,0:T(8,128)(2,1)} %all-gather.12.cloned.1.call-done, f32[292,4096]{1,0:T(8,128)} %fusion.6, f32[292,4096]{1,0:T(8,128)} %fusion.10), kind=kOutput, calls=%fused_computation.19 | convolution fusion | flops 7356493824 | bytes 36528128 | tf_op jit(solution)/shard_map/dot_general | solution.py:58
  1407.1 2.4 reshape.113
  1409.5 3.6 all-to-all-start.3
  1413.2 1.5 reduce-scatter.3.cloned.1.call-done
  1414.7 2.4 reshape.109
  1417.1 9.3 all-to-all-done.3
  1426.5 3.5 all-to-all-start.1
  1430.0 1.0 convert_element_type.56
  1431.5 1.4 convolution_reduce_fusion
  1432.8 9.6 all-to-all-done.1
  1442.7 2.7 multiply_reduce_fusion
  1445.4 3.0 psum.7
  (43 shorter events, 4.5 us)
Async XLA Ops:
  7.2 24.1 %copy-start = (bf16[128,1536]{1,0:T(8,128)(2,1)S(1)}, bf16[128,1536]{1,0:T(8,128)(2,1)}, u32[]{:S(2)}) copy-start(bf16[128,1536]{1,0:T(8,128)(2,1)} %param.10) | copy-start | bytes 1179652
  7.2 44.5 %all-gather.6.cloned.1.call-start = ((), (), s32[]{:S(2)}) async-start(), calls=%async_computation.6 | async-start | bytes 2949120 | tf_op jit(solution)/shard_map/all_gather | solution.py:47
  12.2 20.5 %copy-start.2 = (f32[128,2]{0,1:T(2,128)S(1)}, f32[128,2]{0,1:T(2,128)}, u32[]{:S(2)}) copy-start(f32[128,2]{0,1:T(2,128)} %param.9) | copy-start | bytes 3076
  31.2 28.4 %all-gather.14.cloned.1.call-start = ((), (), s32[]{:S(2)}) async-start(), calls=%async_computation.11 | async-start | bytes 2949120 | tf_op jit(solution)/shard_map/all_gather | solution.py:66
  49.5 438.1 %all-gather.10.cloned.1.call-start = ((), (), s32[]{:S(2)}) async-start(), calls=%async_computation.8 | async-start | bytes 31457280 | tf_op jit(solution)/shard_map/all_gather | solution.py:52
  50.3 862.2 %all-gather.8.cloned.1.call-start = ((), (), s32[]{:S(2)}) async-start(), calls=%async_computation.7 | async-start | bytes 31457280 | tf_op jit(solution)/shard_map/all_gather | solution.py:51
  50.9 1286.4 %all-gather.12.cloned.1.call-start = ((), (), s32[]{:S(2)}) async-start(), calls=%async_computation.9 | async-start | bytes 31457280 | tf_op jit(solution)/shard_map/all_gather | solution.py:57
  51.5 1355.7 %reduce-scatter.5.cloned.1.call-start = ((), (), s32[]{:S(2)}) async-start(), calls=%async_computation.12 | async-start | bytes 2727936 | tf_op jit(solution)/shard_map/reduce_scatter | solution.py:81
  1389.8 24.9 %reduce-scatter.3.cloned.1.call-start = ((), (), s32[]{:S(2)}) async-start(), calls=%async_computation.10 | async-start | bytes 2727936 | tf_op jit(solution)/shard_map/reduce_scatter | solution.py:59
  1407.1 24.1 %copy-start.1 = (s32[128,2]{0,1:T(2,128)S(1)}, s32[128,2]{0,1:T(2,128)}, u32[]{:S(2)}) copy-start(s32[128,2]{0,1:T(2,128)} %param.8) | copy-start | bytes 3076
  1409.5 16.9 %all-to-all-start.3 = ((bf16[4,73,1536]{2,1,0:T(8,128)(2,1)}), bf16[4,73,1536]{2,1,0:T(8,128)(2,1)S(1)}, u32[]{:S(2)}, u32[]{:S(2)}) async-start(bf16[4,73,1536]{2,1,0:T(8,128)(2,1)} %reshape.113), calls=%async_computation.5 | async-start | bytes 1966080 | tf_op jit(solution)/shard_map/all_to_all | solution.py:84
  1426.5 16.0 %all-to-all-start.1 = ((bf16[4,73,1536]{2,1,0:T(8,128)(2,1)}), bf16[4,73,1536]{2,1,0:T(8,128)(2,1)S(1)}, u32[]{:S(2)}, u32[]{:S(2)}) async-start(bf16[4,73,1536]{2,1,0:T(8,128)(2,1)} %reshape.109), calls=%async_computation.2 | async-start | bytes 1966080 | tf_op jit(solution)/shard_map/all_to_all | solution.py:62
Sparse Core Ops, SparseCore 0:
  31.3 9.9 all-gather.5
  49.7 9.9 all-gather.13
  61.2 426.3 all-gather.9
  489.0 423.3 all-gather.7
  913.9 423.3 all-gather.11
  1389.9 7.5 reduce-scatter.4
  1407.2 7.4 reduce-scatter.2
where the time goes:
time: 1460 us
  waiting for transfers between devices  1270 us (87%)
  matrix products  108 us (7%)
  blocking collectives  37.4 us (3%)
  local copies, waits for them, and re-layouts  16.2 us (1%)
    all_gather x1, waiting for transfers between devices, local(): lax.all_gather(up_weight, 'dp', axis=1, tiled=True)  425 us
    all_gather x1, waiting for transfers between devices, local(): down_all = lax.all_gather(down_weight, 'dp', axis=2, tiled=True)  408 us
    all_gather x1, waiting for transfers between devices, local(): lax.all_gather(gate_weight, 'dp', axis=1, tiled=True)  408 us
  transfers between devices with their start and end apart: 9, of which 7 were waited for; matrix products, arithmetic and copies ran while one was open for 4% of the time, Pallas kernels for 0%

commit v1 on v0

--- a/solution.py
+++ b/solution.py
@@ -54,7 +54,21 @@
     gate_pre = jnp.dot(token_rows, gate_all[0], preferred_element_type=jnp.float32)
     up_pre = jnp.dot(token_rows, up_all[0], preferred_element_type=jnp.float32)
     hidden = (jax.nn.silu(gate_pre) * up_pre).astype(jnp.bfloat16)
-    down_all = lax.all_gather(down_weight, "dp", axis=2, tiled=True)
+
+    def sums_all_wrap(field_in):
+        n_peers_all = lax.axis_size("dp")
+        block_out = list(map(lambda nth: (nth - 1, nth), range(1, n_peers_all))) + [
+            (n_peers_all - 1, 0)
+        ]
+        g_now = field_in
+        samples = [g_now]
+        for _ in range(n_peers_all - 1):
+            g_now = lax.ppermute(g_now, axis_name="dp", perm=block_out)
+            samples += [g_now]
+        odd = jnp.concatenate([*reversed(samples)], axis=2)
+        return jnp.roll(odd, shift=(lax.axis_index("dp") + 1) * g_now.shape[2], axis=2)
+
+    down_all = sums_all_wrap(down_weight)
     out_part = jnp.dot(hidden, down_all[0], preferred_element_type=jnp.float32)
     out_sum = lax.psum_scatter(
         out_part.astype(jnp.bfloat16), "tensor", scatter_dimension=1, tiled=True

time: 1460 us -> 1390 us (0.952)
  waiting for transfers between devices: 1270 us -> 992 us
  starting transfers between devices: 7.58 us -> 177 us
  local copies, waits for them, and re-layouts: 16.2 us -> 58 us
    ppermute x0 -> x3, waiting for transfers between devices: none -> 753 us  [sums_all_wrap(): g_now = lax.ppermute(g_now, axis_name='dp', perm=block_out)]
    all_gather x1, waiting for transfers between devices: 425 us -> 0.01 us  [local(): lax.all_gather(up_weight, 'dp', axis=1, tiled=True)]
    all_gather x1 -> x0, waiting for transfers between devices: 408 us -> none  [local(): down_all = lax.all_gather(down_weight, 'dp', axis=2, tiled=True)]
    all_gather x1, waiting for transfers between devices: 408 us -> 217 us  [local(): lax.all_gather(gate_weight, 'dp', axis=1, tiled=True)]
    ppermute x0 -> x3, starting transfers between devices: none -> 169 us  [sums_all_wrap(): g_now = lax.ppermute(g_now, axis_name='dp', perm=block_out)]
    unnamed x8 -> x35, local copies, waits for them, and re-layouts: 0.96 us -> 38.3 us
  transfers between devices with their start and end apart: 9 -> 11, of which waited for: 7 -> 7; matrix products, arithmetic and copies ran while one was open for 4% -> 8% of each run, Pallas kernels for 0% -> 0%
where the time goes in v1:
time: 1390 us
  waiting for transfers between devices  992 us (71%)
  starting transfers between devices  177 us (13%)
  matrix products  109 us (8%)
  local copies, waits for them, and re-layouts  58 us (4%)
  blocking collectives  37.3 us (3%)
  between operations  14.3 us (1%)
    ppermute x3, waiting for transfers between devices, sums_all_wrap(): g_now = lax.ppermute(g_now, axis_name='dp', perm=block_out)  753 us
    all_gather x1, waiting for transfers between devices, local(): lax.all_gather(gate_weight, 'dp', axis=1, tiled=True)  217 us
    ppermute x3, starting transfers between devices, sums_all_wrap(): g_now = lax.ppermute(g_now, axis_name='dp', perm=block_out)  169 us
    unnamed x35, local copies, waits for them, and re-layouts  38.3 us
  transfers between devices with their start and end apart: 11, of which 7 were waited for; matrix products, arithmetic and copies ran while one was open for 8% of the time, Pallas kernels for 0%

profile of v1, /device:TPU:0, one launch (start us, length us, event | category | flops | bytes accessed | tf_op | source)
XLA Modules:
  0.0 1389.9 jit_solution(2359378871206408651)
XLA Ops:
  13.1 18.7 %all_to_all.20 = bf16[4,73,1536]{2,1,0:T(8,128)(2,1)} all-to-all(bf16[4,73,1536]{2,1,0:T(8,128)(2,1)S(1)} %reshape.107), channel_id=1, replica_groups=mesh['expert'=4,'tensor'=2,'dp'=4] {'expert'}, dimensions={0} | all-to-all | bytes 1794048 | tf_op jit(solution)/shard_map/all_to_all | solution.py:46
  34.4 15.6 %all_to_all.21 = bf16[4,73,1536]{2,1,0:T(8,128)(2,1)} all-to-all(bf16[4,73,1536]{2,1,0:T(8,128)(2,1)S(1)} %reshape.111), channel_id=1, replica_groups=mesh['expert'=4,'tensor'=2,'dp'=4] {'expert'}, dimensions={0} | all-to-all | bytes 1794048 | tf_op jit(solution)/shard_map/all_to_all | solution.py:79
  53.1 244.2 %collective-permute-done = bf16[1,4096,768]{2,1,0:T(8,128)(2,1)S(1)} collective-permute-done((bf16[1,4096,768]{2,1,0:T(8,128)(2,1)}, bf16[1,4096,768]{2,1,0:T(8,128)(2,1)S(1)}, u32[]{:S(2)}, u32[]{:S(2)}) %collective-permute-start) | collective-permute-done | bytes 6291488 | tf_op jit(solution)/shard_map/ppermute | solution.py:66
  297.3 2.6 copy-done
  299.8 120.0 %collective-permute-start.1 = (bf16[1,4096,768]{2,1,0:T(8,128)(2,1)S(1)}, bf16[1,4096,768]{2,1,0:T(8,128)(2,1)}, u32[]{:S(2)}, u32[]{:S(2)}) collective-permute-start(bf16[1,4096,768]{2,1,0:T(8,128)(2,1)S(1)} %collective-permute-done), channel_id=1, source_target_pairs={{0,1},{1,2},{2,3},{3,0},{4,5},{5,6},{6,7},{7,4},{8,9},{9,10},{10,1... | collective-permute-start | bytes 18874376 | tf_op jit(solution)/shard_map/ppermute | solution.py:66
  419.9 260.1 %collective-permute-done.1 = bf16[1,4096,768]{2,1,0:T(8,128)(2,1)} collective-permute-done((bf16[1,4096,768]{2,1,0:T(8,128)(2,1)S(1)}, bf16[1,4096,768]{2,1,0:T(8,128)(2,1)}, u32[]{:S(2)}, u32[]{:S(2)}) %collective-permute-start.1) | collective-permute-done | bytes 6291488 | tf_op jit(solution)/shard_map/ppermute | solution.py:66
  680.0 47.8 %collective-permute-start.2 = (bf16[1,4096,768]{2,1,0:T(8,128)(2,1)}, bf16[1,4096,768]{2,1,0:T(8,128)(2,1)}, u32[]{:S(2)}, u32[]{:S(2)}) collective-permute-start(bf16[1,4096,768]{2,1,0:T(8,128)(2,1)} %collective-permute-done.1), channel_id=1, source_target_pairs={{0,1},{1,2},{2,3},{3,0},{4,5},{5,6},{6,7},{7,4},{8,9},{9,10},{10,1... | collective-permute-start | bytes 18874376 | tf_op jit(solution)/shard_map/ppermute | solution.py:66
  727.8 3.3 reshape.108
  731.0 3.4 reshape.112
  734.4 248.7 %collective-permute-done.2 = bf16[1,4096,768]{2,1,0:T(8,128)(2,1)} collective-permute-done((bf16[1,4096,768]{2,1,0:T(8,128)(2,1)}, bf16[1,4096,768]{2,1,0:T(8,128)(2,1)}, u32[]{:S(2)}, u32[]{:S(2)}) %collective-permute-start.2) | collective-permute-done | bytes 6291488 | tf_op jit(solution)/shard_map/ppermute | solution.py:66
  983.1 6.1 constant_dynamic-update-slice_fusion.7
  989.3 6.3 constant_dynamic-update-slice_fusion.6
  995.6 3.1 constant_dynamic-update-slice_fusion.5
  998.6 3.3 constant_dynamic-update-slice_fusion.4
  1001.9 6.2 constant_dynamic-update-slice_fusion.3
  1008.2 5.9 constant_dynamic-update-slice_fusion.2
  1014.1 3.2 constant_dynamic-update-slice_fusion.1
  1017.3 3.1 constant_dynamic-update-slice_fusion
  1020.4 16.1 %fusion = f32[292,4096]{1,0:T(8,128)} fusion(bf16[292,3072]{1,0:T(8,128)(2,1)} %reshape.112, bf16[1,4096,6144]{2,1,0:T(8,128)(2,1)} %constant_dynamic-update-slice_fusion, s32[]{:T(128)S(6)} %select_n.14), kind=kOutput, calls=%fused_computation | convolution fusion | flops 7348420608 | bytes 31768580 | tf_op jit(solution)/shard_map/dot_general | solution.py:83
  1036.5 14.4 %fusion.6 = f32[292,4096]{1,0:T(8,128)} fusion(bf16[292,3072]{1,0:T(8,128)(2,1)S(1)} %copy-done.1, bf16[1,3072,4096]{2,1,0:T(8,128)(2,1)} %all-gather.9.cloned.1.call-done), kind=kOutput, calls=%fused_computation.6 | convolution fusion | flops 7348420608 | bytes 31744000 | tf_op jit(solution)/shard_map/dot_general | solution.py:55
  1050.9 216.8 %all-gather.7.cloned.1.call-done = bf16[1,3072,4096]{2,1,0:T(8,128)(2,1)} async-done(((bf16[1,768,4096]{2,1,0:T(8,128)(2,1)}), bf16[1,3072,4096]{2,1,0:T(8,128)(2,1)}) %all-gather.7.cloned.1.call-update) | async-done | bytes 25165840 | tf_op jit(solution)/shard_map/all_gather | solution.py:51
  1267.8 14.4 %fusion.10 = f32[292,4096]{1,0:T(8,128)} fusion(bf16[292,3072]{1,0:T(8,128)(2,1)S(1)} %copy-done.1, bf16[1,3072,4096]{2,1,0:T(8,128)(2,1)} %all-gather.7.cloned.1.call-done), kind=kOutput, calls=%fused_computation.10 | convolution fusion | flops 7348420608 | bytes 31744000 | tf_op jit(solution)/shard_map/dot_general | solution.py:54
  1282.2 16.7 %fusion.4 = f32[292,3072]{1,0:T(8,128)} fusion(bf16[1,3072,4096]{2,1,0:T(8,128)(2,1)} %all-gather.9.cloned.1.call-done, f32[292,4096]{1,0:T(8,128)} %fusion, f32[292,4096]{1,0:T(8,128)} %fusion.10), kind=kOutput, calls=%fused_computation.4 | convolution fusion | flops 7355596800 | bytes 38322176 | tf_op jit(solution)/shard_map/dot_general | solution.py:92
  1298.8 21.3 %fusion.18 = bf16[292,3072]{1,0:T(8,128)(2,1)} fusion(f32[292,3072]{1,0:T(8,128)} %fusion.4, bf16[1,3072,4096]{2,1,0:T(8,128)(2,1)} %all-gather.7.cloned.1.call-done, f32[292,4096]{1,0:T(8,128)} %fusion.10, f32[292,4096]{1,0:T(8,128)} %fusion, f32[292,4096]{1,0:T(8,128)} %fusion.6), kind=kOutput, calls=%fused_computation.20 | convolution fusion | flops 7362174976 | bytes 44900352 | tf_op jit(solution)/shard_map/dot_general | solution.py:91
  1320.2 21.3 %fusion.21 = bf16[292,3072]{1,0:T(8,128)(2,1)} fusion(bf16[1,4096,6144]{2,1,0:T(8,128)(2,1)} %constant_dynamic-update-slice_fusion, s32[]{:T(128)S(6)} %select_n.14, f32[292,4096]{1,0:T(8,128)} %fusion.6, f32[292,4096]{1,0:T(8,128)} %fusion.10), kind=kOutput, calls=%fused_computation.21 | convolution fusion | flops 7356493824 | bytes 36659204 | tf_op jit(solution)/shard_map/dot_general | solution.py:72
  1341.6 2.4 reshape.113
  1344.1 3.5 all-to-all-start.3
  1350.6 10.4 all-to-all-done.3
  1361.0 3.5 all-to-all-start.1
  1367.4 9.7 all-to-all-done.1
  1377.4 2.7 multiply_reduce_fusion
  1380.1 3.0 psum.7
  (76 shorter events, 17.6 us)
Async XLA Ops:
  7.2 24.7 %copy-start.2 = (bf16[128,1536]{1,0:T(8,128)(2,1)S(1)}, bf16[128,1536]{1,0:T(8,128)(2,1)}, u32[]{:S(2)}) copy-start(bf16[128,1536]{1,0:T(8,128)(2,1)} %param.10) | copy-start | bytes 1179652
  7.2 720.6 %all-gather.5.cloned.1.call-start = ((), (), s32[]{:S(2)}) async-start(), calls=%async_computation.6 | async-start | bytes 2949120 | tf_op jit(solution)/shard_map/all_gather | solution.py:47
  11.7 0.6 copy-start.4
  12.8 20.5 %copy-start.7 = (f32[128,2]{0,1:T(2,128)S(1)}, f32[128,2]{0,1:T(2,128)}, u32[]{:S(2)}) copy-start(f32[128,2]{0,1:T(2,128)} %param.9) | copy-start | bytes 3076
  31.8 699.3 %all-gather.11.cloned.1.call-start = ((), (), s32[]{:S(2)}) async-start(), calls=%async_computation.10 | async-start | bytes 2949120 | tf_op jit(solution)/shard_map/all_gather | solution.py:80
  50.1 986.4 %all-gather.9.cloned.1.call-start = ((), (), s32[]{:S(2)}) async-start(), calls=%async_computation.8 | async-start | bytes 31457280 | tf_op jit(solution)/shard_map/all_gather | solution.py:52
  50.8 1217.0 %all-gather.7.cloned.1.call-start = ((), (), s32[]{:S(2)}) async-start(), calls=%async_computation.7 | async-start | bytes 31457280 | tf_op jit(solution)/shard_map/all_gather | solution.py:51
  51.4 1290.2 %reduce-scatter.5.cloned.1.call-start = ((), (), s32[]{:S(2)}) async-start(), calls=%async_computation.11 | async-start | bytes 2727936 | tf_op jit(solution)/shard_map/reduce_scatter | solution.py:95
  51.4 245.9 %collective-permute-start = (bf16[1,4096,768]{2,1,0:T(8,128)(2,1)}, bf16[1,4096,768]{2,1,0:T(8,128)(2,1)S(1)}, u32[]{:S(2)}, u32[]{:S(2)}) collective-permute-start(bf16[1,4096,768]{2,1,0:T(8,128)(2,1)} %param.13), channel_id=1, source_target_pairs={{0,1},{1,2},{2,3},{3,0},{4,5},{5,6},{6,7},{7,4},{8,9},{9,10},{10,1... | collective-permute-start | bytes 18874376 | tf_op jit(solution)/shard_map/ppermute | solution.py:66
  297.3 2.6 copy-start
  299.8 380.2 %collective-permute-start.1 = (bf16[1,4096,768]{2,1,0:T(8,128)(2,1)S(1)}, bf16[1,4096,768]{2,1,0:T(8,128)(2,1)}, u32[]{:S(2)}, u32[]{:S(2)}) collective-permute-start(bf16[1,4096,768]{2,1,0:T(8,128)(2,1)S(1)} %collective-permute-done), channel_id=1, source_target_pairs={{0,1},{1,2},{2,3},{3,0},{4,5},{5,6},{6,7},{7,4},{8,9},{9,10},{10,1... | collective-permute-start | bytes 18874376 | tf_op jit(solution)/shard_map/ppermute | solution.py:66
  680.0 303.1 %collective-permute-start.2 = (bf16[1,4096,768]{2,1,0:T(8,128)(2,1)}, bf16[1,4096,768]{2,1,0:T(8,128)(2,1)}, u32[]{:S(2)}, u32[]{:S(2)}) collective-permute-start(bf16[1,4096,768]{2,1,0:T(8,128)(2,1)} %collective-permute-done.1), channel_id=1, source_target_pairs={{0,1},{1,2},{2,3},{3,0},{4,5},{5,6},{6,7},{7,4},{8,9},{9,10},{10,1... | collective-permute-start | bytes 18874376 | tf_op jit(solution)/shard_map/ppermute | solution.py:66
  731.0 264.5 %slice-start.2 = ((s8[6291456]{0:T(1024)(128)(4,1)}), s8[2097152]{0:T(1024)(128)(4,1)S(1)}, s32[]{:S(2)}) async-start(s8[6291456]{0:T(1024)(128)(4,1)} %bitcast.54), calls=%async_computation.14 | async-start | bytes 4194304
  734.4 261.1 %slice-start.3 = ((s8[6291456]{0:T(1024)(128)(4,1)}), s8[4194304]{0:T(1024)(128)(4,1)S(1)}, s32[]{:S(2)}) async-start(s8[6291456]{0:T(1024)(128)(4,1)} %bitcast.54), calls=%async_computation.15 | async-start | bytes 8388608
  989.2 9.4 slice-start
  995.6 3.1 slice-start.1
  1020.4 16.1 %copy-start.1 = (bf16[292,3072]{1,0:T(8,128)(2,1)S(1)}, bf16[292,3072]{1,0:T(8,128)(2,1)}, u32[]{:S(2)}) copy-start(bf16[292,3072]{1,0:T(8,128)(2,1)} %reshape.108) | copy-start | bytes 5382148
  1320.2 28.0 %reduce-scatter.3.cloned.1.call-start = ((), (), s32[]{:S(2)}) async-start(), calls=%async_computation.9 | async-start | bytes 2727936 | tf_op jit(solution)/shard_map/reduce_scatter | solution.py:73
  1341.5 23.0 %copy-start.3 = (bf16[128,1536]{1,0:T(8,128)(2,1)S(1)}, bf16[128,1536]{1,0:T(8,128)(2,1)}, u32[]{:S(2)}) copy-start(bf16[128,1536]{1,0:T(8,128)(2,1)} %param.10) | copy-start | bytes 1179652
  1341.5 24.0 %copy-start.5 = (s32[256]{0:T(256)S(1)}, s32[256]{0:T(256)}, u32[]{:S(2)}) copy-start(s32[256]{0:T(256)} %copy-done.4) | copy-start | bytes 3076
  1341.6 24.2 %copy-start.6 = (s32[128,2]{0,1:T(2,128)S(1)}, s32[128,2]{0,1:T(2,128)}, u32[]{:S(2)}) copy-start(s32[128,2]{0,1:T(2,128)} %param.8) | copy-start | bytes 3076
  1344.1 17.0 %all-to-all-start.3 = ((bf16[4,73,1536]{2,1,0:T(8,128)(2,1)}), bf16[4,73,1536]{2,1,0:T(8,128)(2,1)S(1)}, u32[]{:S(2)}, u32[]{:S(2)}) async-start(bf16[4,73,1536]{2,1,0:T(8,128)(2,1)} %reshape.113), calls=%async_computation.5 | async-start | bytes 1966080 | tf_op jit(solution)/shard_map/all_to_all | solution.py:98
  1347.6 29.8 %copy-start.8 = (f32[128,2]{0,1:T(2,128)S(1)}, f32[128,2]{0,1:T(2,128)}, u32[]{:S(2)}) copy-start(f32[128,2]{0,1:T(2,128)} %param.9) | copy-start | bytes 3076
  1361.0 16.1 %all-to-all-start.1 = ((bf16[4,73,1536]{2,1,0:T(8,128)(2,1)}), bf16[4,73,1536]{2,1,0:T(8,128)(2,1)S(1)}, u32[]{:S(2)}, u32[]{:S(2)}) async-start(bf16[4,73,1536]{2,1,0:T(8,128)(2,1)} %reshape.109), calls=%async_computation.2 | async-start | bytes 1966080 | tf_op jit(solution)/shard_map/all_to_all | solution.py:76
Sparse Core Ops, SparseCore 0:
  31.9 9.9 all-gather.4
  50.2 9.9 all-gather.10
  61.7 667.5 all-gather.8
  730.8 536.9 all-gather.6
  1320.3 6.7 reduce-scatter.4
  1341.7 6.4 reduce-scatter.2
